TPU v7x, 32 devices: a whole 2x2x4 slice. The times are simulated.
32 devices in a mesh: groups: 2 (over x), tensor: 2 (over core), query: 8 (over z, y).
Axes of the slice: x: 2, y: 2, z: 4, core: 2. Of those that a mesh axis runs over, the one named last changes fastest.
Arguments:
- query_tokens: bfloat16 [1024, 1024], P(('groups', 'tensor', 'query')), parts along dimension 0, may hold values from -6 to 6
- ln_gain: float32 [1024], replicated, may hold values from 0.1 to 1.9
- inner_weight: bfloat16 [1024, 65536], P(None, ('tensor', 'query')), may hold values from -0.1875 to 0.1875
- outer_weight: bfloat16 [65536, 1024], P(('tensor', 'query')), may hold values from -0.03125 to 0.03125
- final_gain: float32 [1024], replicated, may hold values from 0.1 to 1.9
- projection: bfloat16 [1024, 128], replicated, may hold values from -0.1875 to 0.1875
- segment_ids: int32 [1024], P('groups'), parts along dimension 0, may hold values from 0 to 31, never falling along the last dimension, each value on 1 to 32 neighbouring positions
- index_vectors: bfloat16 [131072, 128], P(('groups', 'tensor', 'query')), parts along dimension 0, may hold values from -6 to 6
- doc_ids: int32 [131072], P(('groups', 'tensor', 'query')), parts along dimension 0, may hold values from 0 to 127, as said below
Outputs:
- scores: float32 [32, 4096], P(None, ('groups', 'tensor', 'query')), parts along dimension 1
There are 2 independent parts, one for each index of `groups`. A program takes and returns all parts, laid end to end along the dimension named above; an argument that names none is the same for every part. Nothing has to cross between parts.
Inputs may be any that keep to these rules, and one draw needn't show every extreme that they name: `doc_ids`: within each shard of 4096 tokens the slot numbers never fall, start at 0 and leave no slot out up to the shard's largest; some shard uses all 128 slots. `segment_ids`: every query number appears; a query's tokens stand together.
All inputs are finite; a program needn't handle non-finite values.
Results may differ from a plain program's by a relative error of at most 0.0011.
Values may be sent and summed in bfloat16 or wider, within the bound.
No kernel may reach another device: no remote copies, remote signals or barrier semaphores. Data moves between devices by JAX's collectives and lax.ppermute only.
A program may use at most 128 MiB of HBM per device.

v0:
```python
import jax
import jax.numpy as jnp
from jax import lax
from jax.sharding import PartitionSpec as P

DOC_DEV = 128
EPSILON = 1e-06


def rms_rows(values, gain):
    mean_square = jnp.mean(values * values, axis=-1, keepdims=True)
    return values * lax.rsqrt(mean_square + EPSILON) * gain


def project_rows(mixed, final_gain, projection):
    final = rms_rows(mixed, final_gain).astype(jnp.bfloat16)
    projected = jnp.dot(final, projection, preferred_element_type=jnp.float32)
    scaled = projected * lax.rsqrt(jnp.sum(projected * projected, axis=-1, keepdims=True) + EPSILON)
    return scaled.astype(jnp.bfloat16)


def score_block(totals, query_rows, segment_rows, index_vectors, doc_ids, present):
    sims = jnp.einsum("jp,tp->jt", index_vectors, query_rows, preferred_element_type=jnp.float32)
    best = jax.ops.segment_max(sims, doc_ids, num_segments=totals.shape[1])
    best = jnp.where(present[:, None], best, 0.0)
    member = (segment_rows[None, :] == lax.iota(jnp.int32, totals.shape[0])[:, None]).astype(
        jnp.float32
    )
    return totals + jnp.einsum("qt,dt->qd", member, best, precision=lax.Precision.HIGHEST)


def score_rows(totals, query_rows, segment_rows, index_vectors, doc_ids, present):
    count_rows = query_rows.shape[0]
    if count_rows > 512 and count_rows % 512 == 0:
        blocks = count_rows // 512

        def block_step(carry, inputs):
            return (score_block(carry, inputs[0], inputs[1], index_vectors, doc_ids, present), None)

        stacked = (
            query_rows.reshape(blocks, 512, query_rows.shape[1]),
            segment_rows.reshape(blocks, 512),
        )
        totals, unused = lax.scan(block_step, totals, stacked)
        return totals
    return score_block(totals, query_rows, segment_rows, index_vectors, doc_ids, present)


def on_device(
    query_tokens,
    ln_gain,
    inner_weight,
    outer_weight,
    final_gain,
    projection,
    segment_ids,
    index_vectors,
    doc_ids,
):
    queries = segment_ids.shape[0] // 16
    present = jnp.any(doc_ids[:, None] == lax.iota(jnp.int32, DOC_DEV)[None, :], axis=0)
    empty = jnp.zeros((queries, DOC_DEV), jnp.float32)
    gathered = lax.all_gather(query_tokens, ("tensor", "query"), axis=0, tiled=True)
    normed = rms_rows(gathered.astype(jnp.float32), ln_gain).astype(jnp.bfloat16)
    hidden = jnp.maximum(
        jnp.dot(normed, inner_weight, preferred_element_type=jnp.float32), 0.0
    ).astype(jnp.bfloat16)
    own_out = lax.psum_scatter(
        jnp.dot(hidden, outer_weight, preferred_element_type=jnp.float32),
        ("tensor", "query"),
        scatter_dimension=0,
        tiled=True,
    )
    own_vectors = project_rows(query_tokens.astype(jnp.float32) + own_out, final_gain, projection)
    totals = score_rows(
        empty,
        lax.all_gather(own_vectors, ("tensor", "query"), axis=0, tiled=True),
        segment_ids,
        index_vectors,
        doc_ids,
        present,
    )
    lengths = jnp.sum(
        (segment_ids[None, :] == lax.iota(jnp.int32, queries)[:, None]).astype(jnp.float32), axis=1
    )
    return totals / lengths[:, None]


def solution(mesh):
    return jax.shard_map(
        on_device,
        mesh=mesh,
        in_specs=(
            P(("groups", "tensor", "query"), None),
            P(),
            P(None, ("tensor", "query")),
            P(("tensor", "query"), None),
            P(),
            P(),
            P("groups"),
            P(("groups", "tensor", "query"), None),
            P(("groups", "tensor", "query")),
        ),
        out_specs=P(None, ("groups", "tensor", "query")),
        check_vma=False,
    )
```

profile of v0, /device:TPU:1, one launch (start us, length us, event | category | flops | bytes accessed | tf_op | source)
XLA Modules:
  0.0 204.2 jit_solution(15623690360071753148)
XLA Ops:
  6.5 0.0 copy-start
  6.5 0.0 all-gather.2.cloned.1.call-start
  6.5 0.7 all-gather.2.cloned.1.call-update
  7.3 0.0 reduce-scatter.2.cloned.1.call-start
  7.3 42.6 %all-gather.2.cloned.1.call-done = bf16[512,1024]{1,0:T(8,128)(2,1)} async-done(((bf16[32,1024]{1,0:T(8,128)(2,1)}), bf16[512,1024]{1,0:T(8,128)(2,1)}) %all-gather.2.cloned.1.call-update) | async-done | bytes 1048592 | tf_op jit(solution)/shard_map/all_gather | solution.py:63
  49.9 1.5 fusion.2
  51.4 0.0 copy-start.4
  51.4 0.0 copy-start.3
  51.4 0.0 copy-start.1
  51.5 0.0 copy-start.2
  51.5 0.0 copy-start.5
  51.5 16.4 %fusion.18 = f32[512,1024]{1,0:T(8,128)} fusion(bf16[4096,1024]{1,0:T(8,128)(2,1)} %param.12, bf16[1024,4096]{1,0:T(8,128)(2,1)} %param.11, bf16[512,1024]{1,0:T(8,128)(2,1)} %all-gather.2.cloned.1.call-done, f32[1024]{0:T(1024)} %param.10, f32[512]{0:T(512)S(1)} %add_rsqrt_fusion), kind=kOutput, calls=%fused_computation.33 | convolution fusion | flops 8596226048 | bytes 19929088 | tf_op jit(solution)/shard_map/dot_general | solution.py:69
  67.9 0.0 reduce-scatter.2.cloned.1.call-update
  67.9 0.0 copy-done.4
  67.9 0.1 convert_reduce_fusion
  68.0 0.0 copy-done.3
  68.0 1.9 fusion.5
  69.9 56.7 %reduce-scatter.2.cloned.1.call-done = f32[32,1024]{1,0:T(8,128)} async-done(((f32[512,1024]{1,0:T(8,128)}), f32[32,1024]{1,0:T(8,128)}) %reduce-scatter.2.cloned.1.call-update) | async-done | bytes 131088 | tf_op jit(solution)/shard_map/reduce_scatter | solution.py:68
  126.6 0.0 copy-done.1
  126.6 1.0 multiply_reduce_fusion
  127.6 0.0 copy-done.2
  127.7 0.0 copy-done.5
  127.7 1.2 multiply_reduce_fusion.1
  128.9 0.1 multiply_convert_fusion.2
  129.0 33.3 %all_gather.7 = bf16[512,128]{1,0:T(8,128)(2,1)S(1)} all-gather(bf16[32,128]{1,0:T(8,128)(2,1)S(1)} %multiply_convert_fusion.2), channel_id=1, replica_groups=mesh['groups'=2,'tensor'=2,'query'=8] {'tensor','query'}, dimensions={0}, use_global_device_ids=true | all-gather | bytes 139264 | tf_op jit(solution)/shard_map/all_gather | solution.py:77
  162.3 0.0 copy-done
  162.3 4.5 %fusion.19 = f32[512,4096]{0,1:T(8,128)} fusion(bf16[512,128]{1,0:T(8,128)(2,1)S(1)} %all_gather.7, bf16[4096,128]{1,0:T(8,128)(2,1)S(1)} %copy-done), kind=kOutput, calls=%fused_computation.34 | convolution fusion | flops 536870912 | bytes 9568256 | tf_op jit(solution)/shard_map/jp,tp->jt/dot_general | solution.py:23
  166.8 29.6 %scatter_custom_fusion = f32[128,512]{1,0:T(8,128)S(1)} fusion(s32[4096]{0:T(1024)S(1)} %copy-done.3, f32[512,4096]{0,1:T(8,128)} %fusion.19, f32[]{:T(128)} %constant.6.clone.1), kind=kCustom, calls=%fused_computation.1 | custom fusion | flops 2097152 | bytes 8650756 | tf_op jit(solution)/shard_map/scatter-max | solution.py:24
  196.4 0.9 convolution_divide_fusion
  (3 shorter events, 0.0 us)
Async XLA Ops:
  6.5 155.8 %copy-start = (bf16[4096,128]{1,0:T(8,128)(2,1)S(1)}, bf16[4096,128]{1,0:T(8,128)(2,1)}, u32[]{:S(2)}) copy-start(bf16[4096,128]{1,0:T(8,128)(2,1)} %param.16) | copy-start | bytes 3145732
  6.5 43.4 %all-gather.2.cloned.1.call-start = ((), (), s32[]{:S(2)}) async-start(), calls=%async_computation.1 | async-start | bytes 1114112 | tf_op jit(solution)/shard_map/all_gather | solution.py:63
  7.3 119.3 %reduce-scatter.2.cloned.1.call-start = ((), (), s32[]{:S(2)}) async-start(), calls=%async_computation.2 | async-start | bytes 2228224 | tf_op jit(solution)/shard_map/reduce_scatter | solution.py:68
  51.4 16.5 %copy-start.4 = (s32[512]{0:T(512)S(1)}, s32[512]{0:T(512)}, u32[]{:S(2)}) copy-start(s32[512]{0:T(512)} %param.15) | copy-start | bytes 6148
  51.4 16.6 %copy-start.3 = (s32[4096]{0:T(1024)S(1)}, s32[4096]{0:T(1024)}, u32[]{:S(2)}) copy-start(s32[4096]{0:T(1024)} %param.17) | copy-start | bytes 49156
  51.4 75.2 %copy-start.1 = (bf16[32,1024]{1,0:T(8,128)(2,1)S(1)}, bf16[32,1024]{1,0:T(8,128)(2,1)}, u32[]{:S(2)}) copy-start(bf16[32,1024]{1,0:T(8,128)(2,1)} %param.9) | copy-start | bytes 196612
  51.5 76.2 %copy-start.2 = (bf16[1024,128]{1,0:T(8,128)(2,1)S(1)}, bf16[1024,128]{1,0:T(8,128)(2,1)}, u32[]{:S(2)}) copy-start(bf16[1024,128]{1,0:T(8,128)(2,1)} %param.14) | copy-start | bytes 786436
  51.5 76.2 %copy-start.5 = (f32[1024]{0:T(1024)S(1)}, f32[1024]{0:T(1024)}, u32[]{:S(2)}) copy-start(f32[1024]{0:T(1024)} %param.13) | copy-start | bytes 12292
Sparse Core Ops, SparseCore 0:
  9.5 40.3 all-gather.1
  68.0 58.5 reduce-scatter.1
where the time goes:
time: 204 us
  waiting for transfers between devices  100 us (49%)
  other arithmetic  34.2 us (17%)
  blocking collectives  33.3 us (16%)
  matrix products  23.1 us (11%)
  between operations  13.5 us (7%)
    reduce_scatter x1, waiting for transfers between devices, on_device(): lax.psum_scatter(jnp.dot(hidden, outer_weight, preferred_element_type=jnp...  56.7 us
    all_gather x1, waiting for transfers between devices, on_device(): lax.all_gather(query_tokens, ('tensor', 'query'), axis=0, tiled=True)  42.6 us
    all_gather x1, blocking collectives, on_device(): lax.all_gather(own_vectors, ('tensor', 'query'), axis=0, tiled=True)  33.3 us
    another operation x1, other arithmetic, score_block(): best = jax.ops.segment_max(sims, doc_ids, num_segments=totals.shape[1])  29.6 us
    dot_general x1, matrix products, on_device(): jnp.dot(hidden, outer_weight, preferred_element_type=jnp.float32)  16.4 us
    dot_general x1, matrix products, score_block(): jnp.einsum('jp,tp->jt', index_vectors, query_rows, preferred_element_type...  4.47 us
  transfers between devices with their start and end apart: 2, of which 2 were waited for; matrix products, arithmetic and copies ran while one was open for 1% of the time, Pallas kernels for 0%

commit v1 on v0

--- a/solution.py
+++ b/solution.py
@@ -5,6 +5,22 @@
 
 DOC_DEV = 128
 EPSILON = 1e-06
+
+
+def ring_gather(x, axis, dim):
+    ways, here, step = (lax.axis_size(axis), lax.axis_index(axis), x.shape[dim])
+    lengths = [n * ways if d == dim else n for d, n in enumerate(x.shape)]
+    full = lax.dynamic_update_slice_in_dim(jnp.zeros(lengths, x.dtype), x, here * step, axis=dim)
+    going_up = going_down = x
+    for far in range(1, ways // 2 + 1):
+        going_up = lax.ppermute(going_up, axis, [(d, (d + 1) % ways) for d in range(ways)])
+        full = lax.dynamic_update_slice_in_dim(full, going_up, (here - far) % ways * step, axis=dim)
+        if 2 * far < ways:
+            going_down = lax.ppermute(going_down, axis, [(d, (d - 1) % ways) for d in range(ways)])
+            full = lax.dynamic_update_slice_in_dim(
+                full, going_down, (here + far) % ways * step, axis=dim
+            )
+    return full
 
 
 def rms_rows(values, gain):
@@ -74,7 +90,7 @@
     own_vectors = project_rows(query_tokens.astype(jnp.float32) + own_out, final_gain, projection)
     totals = score_rows(
         empty,
-        lax.all_gather(own_vectors, ("tensor", "query"), axis=0, tiled=True),
+        ring_gather(own_vectors, ("tensor", "query"), 0),
         segment_ids,
         index_vectors,
         doc_ids,

time: 204 us -> 220 us (1.078); the launches traced: 204 us -> 217 us
  blocking collectives: 33.3 us -> 0 us
  starting transfers between devices: 0.04 us -> 31.2 us
  waiting for transfers between devices: 100 us -> 115 us
    all_gather x1 -> x0, blocking collectives: 33.3 us -> none  [on_device(): lax.all_gather(own_vectors, ('tensor', 'query'), axis=0, tiled=True)]
    ppermute x0 -> x15, starting transfers between devices: none -> 31.1 us  [the longest x7 30.3 us: ring_gather(): lax.ppermute(going_down, axis, [(d, (d - 1) % ways) for d in range(ways)])]
    ppermute x0 -> x15, waiting for transfers between devices: none -> 15 us  [the longest x8 14.9 us: ring_gather(): lax.ppermute(going_up, axis, [(d, (d + 1) % ways) for d in range(ways)])]
  transfers between devices with their start and end apart: 2 -> 17, of which waited for: 2 -> 10; matrix products, arithmetic and copies ran while one was open for 1% -> 1% of each run, Pallas kernels for 0% -> 0%
where the time goes in v1:
time: 220 us; the launch traced here: 217 us
  waiting for transfers between devices  115 us (52%)
  other arithmetic  34.5 us (16%)
  starting transfers between devices  31.2 us (14%)
  matrix products  23.1 us (10%)
  between operations  13.6 us (6%)
    reduce_scatter x1, waiting for transfers between devices, on_device(): lax.psum_scatter(jnp.dot(hidden, outer_weight, preferred_element_type=jnp...  56.6 us
    all_gather x1, waiting for transfers between devices, on_device(): lax.all_gather(query_tokens, ('tensor', 'query'), axis=0, tiled=True)  42.6 us
    ppermute x7, starting transfers between devices, ring_gather(): lax.ppermute(going_down, axis, [(d, (d - 1) % ways) for d in range(ways)])  30.3 us
    another operation x1, other arithmetic, score_block(): best = jax.ops.segment_max(sims, doc_ids, num_segments=totals.shape[1])  29.9 us
    dot_general x1, matrix products, on_device(): jnp.dot(hidden, outer_weight, preferred_element_type=jnp.float32)  16.4 us
    ppermute x8, waiting for transfers between devices, ring_gather(): lax.ppermute(going_up, axis, [(d, (d + 1) % ways) for d in range(ways)])  14.9 us
    dot_general x1, matrix products, score_block(): jnp.einsum('jp,tp->jt', index_vectors, query_rows, preferred_element_type...  4.49 us
  transfers between devices with their start and end apart: 17, of which 10 were waited for; matrix products, arithmetic and copies ran while one was open for 1% of the time, Pallas kernels for 0%

profile of v1, /device:TPU:1, one launch (start us, length us, event | category | flops | bytes accessed | tf_op | source)
XLA Modules:
  0.0 217.4 jit_solution(15969977587433808642)
XLA Ops:
  6.5 0.7 all-gather.2.cloned.1.call-update
  7.3 0.0 reduce-scatter.2.cloned.1.call-start
  7.3 42.6 %all-gather.2.cloned.1.call-done = bf16[512,1024]{1,0:T(8,128)(2,1)} async-done(((bf16[32,1024]{1,0:T(8,128)(2,1)}), bf16[512,1024]{1,0:T(8,128)(2,1)}) %all-gather.2.cloned.1.call-update) | async-done | bytes 1048592 | tf_op jit(solution)/shard_map/all_gather | solution.py:79
  49.9 1.5 fusion.2
  51.4 0.0 copy-start.4
  51.4 0.0 copy-start.3
  51.4 0.0 copy-start.1
  51.5 0.0 copy-start.2
  51.5 0.0 copy-start.5
  51.5 16.4 %fusion.18 = f32[512,1024]{1,0:T(8,128)} fusion(bf16[4096,1024]{1,0:T(8,128)(2,1)} %param.12, bf16[1024,4096]{1,0:T(8,128)(2,1)} %param.11, bf16[512,1024]{1,0:T(8,128)(2,1)} %all-gather.2.cloned.1.call-done, f32[1024]{0:T(1024)} %param.10, f32[512]{0:T(512)S(1)} %add_rsqrt_fusion), kind=kOutput, calls=%fused_computation.49 | convolution fusion | flops 8596226048 | bytes 19929088 | tf_op jit(solution)/shard_map/dot_general | solution.py:85
  67.9 0.0 reduce-scatter.2.cloned.1.call-update
  68.0 0.1 convert_reduce_fusion
  68.1 1.9 fusion.5
  70.0 56.6 %reduce-scatter.2.cloned.1.call-done = f32[32,1024]{1,0:T(8,128)} async-done(((f32[512,1024]{1,0:T(8,128)}), f32[32,1024]{1,0:T(8,128)}) %reduce-scatter.2.cloned.1.call-update) | async-done | bytes 131088 | tf_op jit(solution)/shard_map/reduce_scatter | solution.py:84
  126.6 1.0 multiply_reduce_fusion
  127.7 1.2 multiply_reduce_fusion.1
  128.9 0.1 constant_dynamic-update-slice_fusion.15
  129.0 0.8 collective-permute-start
  129.8 3.7 %collective-permute-start.1 = (bf16[32,128]{1,0:T(8,128)(2,1)S(1)}, bf16[32,128]{1,0:T(8,128)(2,1)S(1)}, u32[]{:S(2)}, u32[]{:S(2)}) collective-permute-start(bf16[32,128]{1,0:T(8,128)(2,1)S(1)} %get-tuple-element.6), channel_id=1, source_target_pairs={{0,15},{1,0},{2,1},{3,2},{4,3},{5,4},{6,5},{7,6},{8,7},{9,8},{10,9... | collective-permute-start | bytes 24584 | tf_op jit(solution)/shard_map/ppermute | solution.py:19
  133.5 1.3 collective-permute-done
  134.8 0.0 collective-permute-start.2
  134.8 0.0 collective-permute-done.1
  134.8 4.4 %collective-permute-start.3 = (bf16[32,128]{1,0:T(8,128)(2,1)S(1)}, bf16[32,128]{1,0:T(8,128)(2,1)S(1)}, u32[]{:S(2)}, u32[]{:S(2)}) collective-permute-start(bf16[32,128]{1,0:T(8,128)(2,1)S(1)} %collective-permute-done.1), channel_id=1, source_target_pairs={{0,15},{1,0},{2,1},{3,2},{4,3},{5,4},{6,5},{7,6},{8,7},{9,8},{10,9... | collective-permute-start | bytes 24584 | tf_op jit(solution)/shard_map/ppermute | solution.py:19
  139.3 1.3 collective-permute-done.2
  140.6 0.0 collective-permute-start.4
  140.6 0.0 collective-permute-done.3
  140.6 4.4 %collective-permute-start.5 = (bf16[32,128]{1,0:T(8,128)(2,1)S(1)}, bf16[32,128]{1,0:T(8,128)(2,1)S(1)}, u32[]{:S(2)}, u32[]{:S(2)}) collective-permute-start(bf16[32,128]{1,0:T(8,128)(2,1)S(1)} %collective-permute-done.3), channel_id=1, source_target_pairs={{0,15},{1,0},{2,1},{3,2},{4,3},{5,4},{6,5},{7,6},{8,7},{9,8},{10,9... | collective-permute-start | bytes 24584 | tf_op jit(solution)/shard_map/ppermute | solution.py:19
  145.0 1.3 collective-permute-done.4
  146.3 0.0 collective-permute-start.6
  146.4 0.0 collective-permute-done.5
  146.4 4.4 %collective-permute-start.7 = (bf16[32,128]{1,0:T(8,128)(2,1)S(1)}, bf16[32,128]{1,0:T(8,128)(2,1)S(1)}, u32[]{:S(2)}, u32[]{:S(2)}) collective-permute-start(bf16[32,128]{1,0:T(8,128)(2,1)S(1)} %collective-permute-done.5), channel_id=1, source_target_pairs={{0,15},{1,0},{2,1},{3,2},{4,3},{5,4},{6,5},{7,6},{8,7},{9,8},{10,9... | collective-permute-start | bytes 24584 | tf_op jit(solution)/shard_map/ppermute | solution.py:19
  150.8 1.3 collective-permute-done.6
  152.1 0.0 collective-permute-start.8
  152.1 0.0 collective-permute-done.7
  152.1 4.4 %collective-permute-start.9 = (bf16[32,128]{1,0:T(8,128)(2,1)S(1)}, bf16[32,128]{1,0:T(8,128)(2,1)S(1)}, u32[]{:S(2)}, u32[]{:S(2)}) collective-permute-start(bf16[32,128]{1,0:T(8,128)(2,1)S(1)} %collective-permute-done.7), channel_id=1, source_target_pairs={{0,15},{1,0},{2,1},{3,2},{4,3},{5,4},{6,5},{7,6},{8,7},{9,8},{10,9... | collective-permute-start | bytes 24584 | tf_op jit(solution)/shard_map/ppermute | solution.py:19
  156.6 1.3 collective-permute-done.8
  157.9 0.0 collective-permute-start.10
  157.9 0.0 collective-permute-done.9
  157.9 4.4 %collective-permute-start.11 = (bf16[32,128]{1,0:T(8,128)(2,1)S(1)}, bf16[32,128]{1,0:T(8,128)(2,1)S(1)}, u32[]{:S(2)}, u32[]{:S(2)}) collective-permute-start(bf16[32,128]{1,0:T(8,128)(2,1)S(1)} %collective-permute-done.9), channel_id=1, source_target_pairs={{0,15},{1,0},{2,1},{3,2},{4,3},{5,4},{6,5},{7,6},{8,7},{9,8},{10,9... | collective-permute-start | bytes 24584 | tf_op jit(solution)/shard_map/ppermute | solution.py:19
  162.4 1.3 collective-permute-done.10
  163.7 0.0 collective-permute-done.11
  163.7 4.4 %collective-permute-start.13 = (bf16[32,128]{1,0:T(8,128)(2,1)S(1)}, bf16[32,128]{1,0:T(8,128)(2,1)S(1)}, u32[]{:S(2)}, u32[]{:S(2)}) collective-permute-start(bf16[32,128]{1,0:T(8,128)(2,1)S(1)} %collective-permute-done.11), channel_id=1, source_target_pairs={{0,15},{1,0},{2,1},{3,2},{4,3},{5,4},{6,5},{7,6},{8,7},{9,8},{10,9... | collective-permute-start | bytes 24584 | tf_op jit(solution)/shard_map/ppermute | solution.py:19
  168.1 1.3 collective-permute-done.12
  169.4 0.0 collective-permute-start.14
  169.5 5.7 %collective-permute-done.14 = bf16[32,128]{1,0:T(8,128)(2,1)S(1)} collective-permute-done((bf16[32,128]{1,0:T(8,128)(2,1)S(1)}, bf16[32,128]{1,0:T(8,128)(2,1)S(1)}, u32[]{:S(2)}, u32[]{:S(2)}) %collective-permute-start.14) | collective-permute-done | bytes 8224 | tf_op jit(solution)/shard_map/ppermute | solution.py:16
  175.2 4.5 %fusion.19 = f32[512,4096]{0,1:T(8,128)} fusion(bf16[512,128]{1,0:T(8,128)(2,1)S(1)} %constant_dynamic-update-slice_fusion, bf16[4096,128]{1,0:T(8,128)(2,1)S(1)} %copy-done), kind=kOutput, calls=%fused_computation.50 | convolution fusion | flops 536870912 | bytes 9568256 | tf_op jit(solution)/shard_map/jp,tp->jt/dot_general | solution.py:39
  179.7 29.9 %scatter_custom_fusion = f32[128,512]{1,0:T(8,128)S(1)} fusion(s32[4096]{0:T(1024)S(1)} %copy-done.3, f32[512,4096]{0,1:T(8,128)} %fusion.19, f32[]{:T(128)} %constant.103.clone.1), kind=kCustom, calls=%fused_computation.1 | custom fusion | flops 2097152 | bytes 8650756 | tf_op jit(solution)/shard_map/scatter-max | solution.py:40
  209.6 0.9 convolution_divide_fusion
  (29 shorter events, 0.2 us)
Async XLA Ops:
  6.5 168.7 %copy-start = (bf16[4096,128]{1,0:T(8,128)(2,1)S(1)}, bf16[4096,128]{1,0:T(8,128)(2,1)}, u32[]{:S(2)}) copy-start(bf16[4096,128]{1,0:T(8,128)(2,1)} %param.16) | copy-start | bytes 3145732
  6.5 43.4 %all-gather.2.cloned.1.call-start = ((), (), s32[]{:S(2)}) async-start(), calls=%async_computation.1 | async-start | bytes 1114112 | tf_op jit(solution)/shard_map/all_gather | solution.py:79
  7.3 119.3 %reduce-scatter.2.cloned.1.call-start = ((), (), s32[]{:S(2)}) async-start(), calls=%async_computation.2 | async-start | bytes 2228224 | tf_op jit(solution)/shard_map/reduce_scatter | solution.py:84
  51.4 16.6 %copy-start.4 = (s32[512]{0:T(512)S(1)}, s32[512]{0:T(512)}, u32[]{:S(2)}) copy-start(s32[512]{0:T(512)} %param.15) | copy-start | bytes 6148
  51.4 16.7 %copy-start.3 = (s32[4096]{0:T(1024)S(1)}, s32[4096]{0:T(1024)}, u32[]{:S(2)}) copy-start(s32[4096]{0:T(1024)} %param.17) | copy-start | bytes 49156
  51.4 75.1 %copy-start.1 = (bf16[32,1024]{1,0:T(8,128)(2,1)S(1)}, bf16[32,1024]{1,0:T(8,128)(2,1)}, u32[]{:S(2)}) copy-start(bf16[32,1024]{1,0:T(8,128)(2,1)} %param.9) | copy-start | bytes 196612
  51.5 76.2 %copy-start.2 = (bf16[1024,128]{1,0:T(8,128)(2,1)S(1)}, bf16[1024,128]{1,0:T(8,128)(2,1)}, u32[]{:S(2)}) copy-start(bf16[1024,128]{1,0:T(8,128)(2,1)} %param.14) | copy-start | bytes 786436
  51.5 76.2 %copy-start.5 = (f32[1024]{0:T(1024)S(1)}, f32[1024]{0:T(1024)}, u32[]{:S(2)}) copy-start(f32[1024]{0:T(1024)} %param.13) | copy-start | bytes 12292
  129.0 5.8 %collective-permute-start = (bf16[32,128]{1,0:T(8,128)(2,1)S(1)}, bf16[32,128]{1,0:T(8,128)(2,1)S(1)}, u32[]{:S(2)}, u32[]{:S(2)}) collective-permute-start(bf16[32,128]{1,0:T(8,128)(2,1)S(1)} %get-tuple-element.6), channel_id=1, source_target_pairs={{0,1},{1,2},{2,3},{3,4},{4,5},{5,6},{6,7},{7,8},{8,9},{9,10},{10,1... | collective-permute-start | bytes 24584 | tf_op jit(solution)/shard_map/ppermute | solution.py:16
  129.8 5.0 %collective-permute-start.1 = (bf16[32,128]{1,0:T(8,128)(2,1)S(1)}, bf16[32,128]{1,0:T(8,128)(2,1)S(1)}, u32[]{:S(2)}, u32[]{:S(2)}) collective-permute-start(bf16[32,128]{1,0:T(8,128)(2,1)S(1)} %get-tuple-element.6), channel_id=1, source_target_pairs={{0,15},{1,0},{2,1},{3,2},{4,3},{5,4},{6,5},{7,6},{8,7},{9,8},{10,9... | collective-permute-start | bytes 24584 | tf_op jit(solution)/shard_map/ppermute | solution.py:19
  134.8 5.8 %collective-permute-start.2 = (bf16[32,128]{1,0:T(8,128)(2,1)S(1)}, bf16[32,128]{1,0:T(8,128)(2,1)S(1)}, u32[]{:S(2)}, u32[]{:S(2)}) collective-permute-start(bf16[32,128]{1,0:T(8,128)(2,1)S(1)} %collective-permute-done), channel_id=1, source_target_pairs={{0,1},{1,2},{2,3},{3,4},{4,5},{5,6},{6,7},{7,8},{8,9},{9,10},{10,1... | collective-permute-start | bytes 24584 | tf_op jit(solution)/shard_map/ppermute | solution.py:16
  134.8 5.8 %collective-permute-start.3 = (bf16[32,128]{1,0:T(8,128)(2,1)S(1)}, bf16[32,128]{1,0:T(8,128)(2,1)S(1)}, u32[]{:S(2)}, u32[]{:S(2)}) collective-permute-start(bf16[32,128]{1,0:T(8,128)(2,1)S(1)} %collective-permute-done.1), channel_id=1, source_target_pairs={{0,15},{1,0},{2,1},{3,2},{4,3},{5,4},{6,5},{7,6},{8,7},{9,8},{10,9... | collective-permute-start | bytes 24584 | tf_op jit(solution)/shard_map/ppermute | solution.py:19
  140.6 5.8 %collective-permute-start.4 = (bf16[32,128]{1,0:T(8,128)(2,1)S(1)}, bf16[32,128]{1,0:T(8,128)(2,1)S(1)}, u32[]{:S(2)}, u32[]{:S(2)}) collective-permute-start(bf16[32,128]{1,0:T(8,128)(2,1)S(1)} %collective-permute-done.2), channel_id=1, source_target_pairs={{0,1},{1,2},{2,3},{3,4},{4,5},{5,6},{6,7},{7,8},{8,9},{9,10},{10,1... | collective-permute-start | bytes 24584 | tf_op jit(solution)/shard_map/ppermute | solution.py:16
  140.6 5.8 %collective-permute-start.5 = (bf16[32,128]{1,0:T(8,128)(2,1)S(1)}, bf16[32,128]{1,0:T(8,128)(2,1)S(1)}, u32[]{:S(2)}, u32[]{:S(2)}) collective-permute-start(bf16[32,128]{1,0:T(8,128)(2,1)S(1)} %collective-permute-done.3), channel_id=1, source_target_pairs={{0,15},{1,0},{2,1},{3,2},{4,3},{5,4},{6,5},{7,6},{8,7},{9,8},{10,9... | collective-permute-start | bytes 24584 | tf_op jit(solution)/shard_map/ppermute | solution.py:19
  146.3 5.8 %collective-permute-start.6 = (bf16[32,128]{1,0:T(8,128)(2,1)S(1)}, bf16[32,128]{1,0:T(8,128)(2,1)S(1)}, u32[]{:S(2)}, u32[]{:S(2)}) collective-permute-start(bf16[32,128]{1,0:T(8,128)(2,1)S(1)} %collective-permute-done.4), channel_id=1, source_target_pairs={{0,1},{1,2},{2,3},{3,4},{4,5},{5,6},{6,7},{7,8},{8,9},{9,10},{10,1... | collective-permute-start | bytes 24584 | tf_op jit(solution)/shard_map/ppermute | solution.py:16
  146.4 5.8 %collective-permute-start.7 = (bf16[32,128]{1,0:T(8,128)(2,1)S(1)}, bf16[32,128]{1,0:T(8,128)(2,1)S(1)}, u32[]{:S(2)}, u32[]{:S(2)}) collective-permute-start(bf16[32,128]{1,0:T(8,128)(2,1)S(1)} %collective-permute-done.5), channel_id=1, source_target_pairs={{0,15},{1,0},{2,1},{3,2},{4,3},{5,4},{6,5},{7,6},{8,7},{9,8},{10,9... | collective-permute-start | bytes 24584 | tf_op jit(solution)/shard_map/ppermute | solution.py:19
  152.1 5.8 %collective-permute-start.8 = (bf16[32,128]{1,0:T(8,128)(2,1)S(1)}, bf16[32,128]{1,0:T(8,128)(2,1)S(1)}, u32[]{:S(2)}, u32[]{:S(2)}) collective-permute-start(bf16[32,128]{1,0:T(8,128)(2,1)S(1)} %collective-permute-done.6), channel_id=1, source_target_pairs={{0,1},{1,2},{2,3},{3,4},{4,5},{5,6},{6,7},{7,8},{8,9},{9,10},{10,1... | collective-permute-start | bytes 24584 | tf_op jit(solution)/shard_map/ppermute | solution.py:16
  152.1 5.8 %collective-permute-start.9 = (bf16[32,128]{1,0:T(8,128)(2,1)S(1)}, bf16[32,128]{1,0:T(8,128)(2,1)S(1)}, u32[]{:S(2)}, u32[]{:S(2)}) collective-permute-start(bf16[32,128]{1,0:T(8,128)(2,1)S(1)} %collective-permute-done.7), channel_id=1, source_target_pairs={{0,15},{1,0},{2,1},{3,2},{4,3},{5,4},{6,5},{7,6},{8,7},{9,8},{10,9... | collective-permute-start | bytes 24584 | tf_op jit(solution)/shard_map/ppermute | solution.py:19
  157.9 5.8 %collective-permute-start.10 = (bf16[32,128]{1,0:T(8,128)(2,1)S(1)}, bf16[32,128]{1,0:T(8,128)(2,1)S(1)}, u32[]{:S(2)}, u32[]{:S(2)}) collective-permute-start(bf16[32,128]{1,0:T(8,128)(2,1)S(1)} %collective-permute-done.8), channel_id=1, source_target_pairs={{0,1},{1,2},{2,3},{3,4},{4,5},{5,6},{6,7},{7,8},{8,9},{9,10},{10,1... | collective-permute-start | bytes 24584 | tf_op jit(solution)/shard_map/ppermute | solution.py:16
  157.9 5.8 %collective-permute-start.11 = (bf16[32,128]{1,0:T(8,128)(2,1)S(1)}, bf16[32,128]{1,0:T(8,128)(2,1)S(1)}, u32[]{:S(2)}, u32[]{:S(2)}) collective-permute-start(bf16[32,128]{1,0:T(8,128)(2,1)S(1)} %collective-permute-done.9), channel_id=1, source_target_pairs={{0,15},{1,0},{2,1},{3,2},{4,3},{5,4},{6,5},{7,6},{8,7},{9,8},{10,9... | collective-permute-start | bytes 24584 | tf_op jit(solution)/shard_map/ppermute | solution.py:19
  163.7 5.8 %collective-permute-start.12 = (bf16[32,128]{1,0:T(8,128)(2,1)S(1)}, bf16[32,128]{1,0:T(8,128)(2,1)S(1)}, u32[]{:S(2)}, u32[]{:S(2)}) collective-permute-start(bf16[32,128]{1,0:T(8,128)(2,1)S(1)} %collective-permute-done.10), channel_id=1, source_target_pairs={{0,1},{1,2},{2,3},{3,4},{4,5},{5,6},{6,7},{7,8},{8,9},{9,10},{10,1... | collective-permute-start | bytes 24584 | tf_op jit(solution)/shard_map/ppermute | solution.py:16
  163.7 5.8 %collective-permute-start.13 = (bf16[32,128]{1,0:T(8,128)(2,1)S(1)}, bf16[32,128]{1,0:T(8,128)(2,1)S(1)}, u32[]{:S(2)}, u32[]{:S(2)}) collective-permute-start(bf16[32,128]{1,0:T(8,128)(2,1)S(1)} %collective-permute-done.11), channel_id=1, source_target_pairs={{0,15},{1,0},{2,1},{3,2},{4,3},{5,4},{6,5},{7,6},{8,7},{9,8},{10,9... | collective-permute-start | bytes 24584 | tf_op jit(solution)/shard_map/ppermute | solution.py:19
  169.4 5.8 %collective-permute-start.14 = (bf16[32,128]{1,0:T(8,128)(2,1)S(1)}, bf16[32,128]{1,0:T(8,128)(2,1)S(1)}, u32[]{:S(2)}, u32[]{:S(2)}) collective-permute-start(bf16[32,128]{1,0:T(8,128)(2,1)S(1)} %collective-permute-done.12), channel_id=1, source_target_pairs={{0,1},{1,2},{2,3},{3,4},{4,5},{5,6},{6,7},{7,8},{8,9},{9,10},{10,1... | collective-permute-start | bytes 24584 | tf_op jit(solution)/shard_map/ppermute | solution.py:16
Sparse Core Ops, SparseCore 0:
  9.5 40.3 all-gather.1
  68.0 58.5 reduce-scatter.1
